TPU v7x, 32 devices: a whole 2x2x4 slice. The times are simulated.
32 devices in a mesh: frame: 8 (over z, y), row: 4 (over x, core).
Axes of the slice: x: 2, y: 2, z: 4, core: 2. Of those that a mesh axis runs over, the one named last changes fastest.
Arguments:
- frames_x: bfloat16 [8, 24, 128, 512], P('frame', 'row'), may hold values from -6 to 6
- conv_weight: bfloat16 [3, 3, 512, 512], replicated, may hold values from -0.09375 to 0.09375
- conv_bias: float32 [512], replicated, may hold values from -3 to 3
- query_weight: bfloat16 [512, 512], replicated, may hold values from -0.25 to 0.25
- key_weight: bfloat16 [512, 512], replicated, may hold values from -0.25 to 0.25
- value_weight: bfloat16 [512, 512], replicated, may hold values from -0.25 to 0.25
- out_weight: bfloat16 [512, 512], replicated, may hold values from -0.25 to 0.25
- query_gain: float32 [512], replicated, may hold values from 0.5 to 2
- key_gain: float32 [512], replicated, may hold values from 0.5 to 2
- source_ids: int32 [8, 24, 4], P('frame', 'row'), may hold values from 0 to 23, as said below
- valid_counts: int32 [8, 24], P('frame', 'row'), may hold values from 1 to 4
Outputs:
- propagated: bfloat16 [8, 24, 128, 512], P('frame', 'row')
Inputs may be any that keep to these rules, and one draw needn't show every extreme that they name: `source_ids`: block id s names row s // 1 of the previous frame, which lies at most 2 rows from the querying block's row; in every frame slot 0 of the blocks in even rows names a block 2 rows above and in odd rows 2 rows below, as far as the frame has that row.
All inputs are finite; a program needn't handle non-finite values.
Results may differ from a plain program's by a relative error of at most 0.0054.
Values may be sent and summed in bfloat16 or wider, within the bound.
A program may use at most 64 MiB of HBM per device.

v0:
```python
import functools

import jax
import jax.numpy as jnp
from jax import lax
from jax.experimental import pallas as pl
from jax.experimental.pallas import tpu as pltpu
from jax.sharding import PartitionSpec as P

HEADS = 8
HD = 64
KSRC = 4
DISP = 2
GROUP = 4
F32 = jnp.float32
BF16 = jnp.bfloat16


def dot(a, b):
    return jnp.dot(a, b, preferred_element_type=F32)


def shift_columns(left, mid, right, width):
    count = mid.shape[0]
    col = lax.broadcasted_iota(jnp.int32, mid.shape, 0) % width
    return (
        mid
        + jnp.where(col == 0, 0.0, pltpu.roll(left, 1, 0))
        + jnp.where(col == width - 1, 0.0, pltpu.roll(right, count - 1, 0))
    )


def head_mean(chans):
    row = lax.broadcasted_iota(jnp.int32, (chans, chans), 0) // HD
    col = lax.broadcasted_iota(jnp.int32, (chans, chans), 1) // HD
    return jnp.where(row == col, 1.0 / HD, 0.0).astype(BF16)


def normed(feats, weight, gain, mean, scale):
    proj = dot(feats, weight)
    square = dot((proj * proj).astype(BF16), mean)
    out = (proj * lax.rsqrt(square + 1e-06) * gain).astype(BF16)
    return out * scale if scale != 1 else out


def kernel(
    ids, valid, x, wc_hbm, wq_hbm, wk_hbm, wv_hbm, wo_hbm, bias, gq, gk,
    out,
    ext, wc, wq, wk, wv, wo, feats, reach, q, keys, values, mixed, mixture, sums,
    local_sem, send_sem, recv_sem,
):
    rows, width, chans = x.shape
    frame, band = lax.axis_index("frame"), lax.axis_index("row")
    frames, bands = lax.axis_size("frame"), lax.axis_size("row")
    has_prev, has_next = frame > 0, frame < frames - 1
    has_above, has_below = band > 0, band < bands - 1
    to_above, to_below, to_next = {"row": band - 1}, {"row": band + 1}, {"frame": frame + 1}

    def fetch(i, src, dst):
        return pltpu.make_async_copy(src, dst, local_sem.at[i])

    def send(i, src, dst, device):
        return pltpu.make_async_remote_copy(
            src_ref=src,
            dst_ref=dst,
            send_sem=send_sem.at[i],
            recv_sem=recv_sem.at[i],
            device_id=device,
            device_id_type=pl.DeviceIdType.MESH,
        )

    barrier = pltpu.get_barrier_semaphore()
    met = 0
    for there, device in (
        (has_above, to_above),
        (has_below, to_below),
        (has_prev, {"frame": frame - 1}),
        (has_next, to_next),
    ):
        met = met + there.astype(jnp.int32)

        @pl.when(there)
        def _():
            pl.semaphore_signal(
                barrier, inc=1, device_id=device, device_id_type=pl.DeviceIdType.MESH
            )

    load_x = fetch(0, x, ext.at[pl.ds(1, rows)])
    load_x.start()
    taps = [fetch(1 + b, wc_hbm.at[:, b], wc.at[:, b]) for b in range(3)]
    mats = [
        fetch(4 + i, src, dst)
        for i, (src, dst) in enumerate(
            ((wq_hbm, wq), (wk_hbm, wk), (wv_hbm, wv), (wo_hbm, wo))
        )
    ]
    for copy in taps:
        copy.start()

    pl.semaphore_wait(barrier, met)

    halo_up = send(0, x.at[0], ext.at[rows + 1], to_above)
    halo_down = send(1, x.at[rows - 1], ext.at[0], to_below)

    @pl.when(has_above)
    def _():
        halo_up.start()

    @pl.when(has_below)
    def _():
        halo_down.start()

    blank = jnp.zeros((width, chans), BF16)

    @pl.when(band == 0)
    def _():
        ext[0] = blank
        for i in range(DISP):
            reach[i] = blank

    @pl.when(band == bands - 1)
    def _():
        ext[rows + 1] = blank
        for i in range(DISP):
            reach[DISP + rows + i] = blank

    @pl.when(frame == 0)
    def _():
        for i in range(rows + 2 * DISP):
            reach[i] = blank

    spans = ((0, DISP), (rows - DISP, DISP), (DISP, rows - 2 * DISP))
    moves = [
        send(
            2 + i,
            feats.at[pl.ds(start, size)],
            reach.at[pl.ds(DISP + start, size)],
            to_next,
        )
        for i, (start, size) in enumerate(spans)
    ]
    relay_up = send(5, reach.at[pl.ds(DISP, DISP)], reach.at[pl.ds(DISP + rows, DISP)], to_above)
    relay_down = send(6, reach.at[pl.ds(rows, DISP)], reach.at[pl.ds(0, DISP)], to_below)

    load_x.wait()
    for i, (start, size) in enumerate(spans):
        if i == 0:

            @pl.when(has_above)
            def _():
                halo_down.wait_recv()

        if i == 1:

            @pl.when(has_below)
            def _():
                halo_up.wait_recv()

        window = jnp.concatenate(
            [ext[start + a : start + a + size].reshape(size * width, chans) for a in range(3)],
            axis=1,
        )
        parts = []
        for b in range(3):
            if i == 0:
                taps[b].wait()
            parts.append(dot(window, jnp.concatenate([wc[a, b] for a in range(3)], axis=0)))
        total = shift_columns(*parts, width) + bias[...]
        feats[start : start + size] = total.astype(BF16).reshape(size, width, chans)

        @pl.when(has_next)
        def _():
            moves[i].start()

        if i == 0:
            for copy in mats:
                copy.start()

    mean = head_mean(chans)

    def project(src, start, size, place):
        f = src[start : start + size].reshape(size * width, chans)
        blocked = (size, width, chans)
        keys[place : place + size] = normed(f, wk[...], gk[...], mean, 1).reshape(blocked)
        values[place : place + size] = dot(f, wv[...]).astype(BF16).reshape(blocked)

    lanes = GROUP * HD
    head = lax.broadcasted_iota(jnp.int32, (1, lanes), 1) // HD
    slot = lax.broadcasted_iota(jnp.int32, (1, KSRC * width), 1) // width
    base = band * rows - DISP - rows
    live = has_prev.astype(jnp.int32)

    def by_head(stacked):
        joined = stacked[0:width]
        for h in range(1, GROUP):
            joined = jnp.where(head == h, stacked[h * width : (h + 1) * width], joined)
        return joined

    def exponentials(n, cut, key):
        query = q[n, :, cut]
        stack = jnp.concatenate(
            [jnp.where(head == h, query, jnp.zeros_like(query)) for h in range(GROUP)], axis=0
        )
        return jnp.exp(
            lax.dot_general(stack, key, (((1,), (1,)), ((), ())), preferred_element_type=F32)
        )

    def own(n, carry):
        for g in range(chans // lanes):
            cut = pl.ds(g * lanes, lanes)
            expo = exponentials(n, cut, keys[n, :, cut])
            sums[n, g] = expo
            mixture[n, :, cut] = by_head(dot(expo.astype(BF16), values[n, :, cut]))
        return carry

    def block(n, carry):
        places = [
            jnp.clip(ids[0, j, n] - base, rows, 2 * rows + 2 * DISP - 1) for j in range(KSRC)
        ]
        mask = slot < valid[0, n] * live
        for g in range(chans // lanes):
            cut = pl.ds(g * lanes, lanes)
            key = jnp.concatenate([keys[p, :, cut] for p in places], axis=0)
            value = jnp.concatenate([values[p, :, cut] for p in places], axis=0)
            expo = jnp.where(mask, exponentials(n, cut, key), 0.0)
            folded = sums[n, g]
            for j in range(KSRC):
                folded = folded + expo[:, j * width : (j + 1) * width]
            inverse = 1.0 / jnp.sum(folded, axis=1, keepdims=True)
            part = by_head(dot(expo.astype(BF16), value)) + mixture[n, :, cut]
            mixed[n, :, cut] = (part * by_head(inverse)).astype(BF16)
        return carry

    for copy in mats:
        copy.wait()
    flat = feats[...].reshape(rows * width, chans)
    q[...] = normed(flat, wq[...], gq[...], mean, HD**-0.5).reshape(rows, width, chans)
    project(feats, 0, rows, 0)

    @pl.when(has_prev)
    def _():
        moves[0].wait_recv()

    @pl.when(has_prev & has_above)
    def _():
        relay_up.start()

    project(reach, DISP, DISP, rows + DISP)
    lax.fori_loop(0, rows, own, 0, unroll=True)

    @pl.when(has_prev)
    def _():
        moves[1].wait_recv()

    @pl.when(has_prev & has_below)
    def _():
        relay_down.start()

    project(reach, rows, DISP, 2 * rows)

    @pl.when(has_prev & has_above)
    def _():
        relay_down.wait_recv()

    project(reach, 0, DISP, rows)

    @pl.when(has_prev & has_below)
    def _():
        relay_up.wait_recv()

    project(reach, DISP + rows, DISP, 2 * rows + DISP)

    @pl.when(has_prev)
    def _():
        moves[2].wait_recv()

    project(reach, 2 * DISP, rows - 2 * DISP, rows + 2 * DISP)

    lax.fori_loop(0, rows, block, 0, unroll=True)
    flat = mixed[...].reshape(rows * width, chans)
    f = feats[...].reshape(rows * width, chans).astype(F32)
    out[...] = (f + dot(flat, wo[...])).astype(BF16).reshape(rows, width, chans)

    @pl.when(has_above)
    def _():
        halo_up.wait_send()

    @pl.when(has_below)
    def _():
        halo_down.wait_send()

    for copy in moves:

        @pl.when(has_next)
        def _():
            copy.wait_send()

    @pl.when(has_prev & has_above)
    def _():
        relay_up.wait_send()

    @pl.when(has_prev & has_below)
    def _():
        relay_down.wait_send()


VM = pl.BlockSpec(memory_space=pltpu.VMEM)
SM = pl.BlockSpec(memory_space=pltpu.SMEM)
ANY = pl.BlockSpec(memory_space=pl.ANY)


def shards(x, wc, bias, wq, wk, wv, wo, gq, gk, source_ids, valid_counts):
    x = x[0]
    rows, width, chans = x.shape
    square = pltpu.VMEM((chans, chans), BF16)

    def stack(count):
        return pltpu.VMEM((count, width, chans), BF16)

    out = pl.pallas_call(
        kernel,
        out_shape=jax.ShapeDtypeStruct((rows, width, chans), BF16),
        in_specs=[SM, SM] + [ANY] * 6 + [VM] * 3,
        out_specs=VM,
        scratch_shapes=[
            stack(rows + 2),
            pltpu.VMEM(wc.shape, BF16),
            square,
            square,
            square,
            square,
            stack(rows),
            stack(rows + 2 * DISP),
            stack(rows),
            stack(2 * rows + 2 * DISP),
            stack(2 * rows + 2 * DISP),
            stack(rows),
            pltpu.VMEM((rows, width, chans), F32),
            pltpu.VMEM((rows, chans // (GROUP * HD), GROUP * width, width), F32),
            pltpu.SemaphoreType.DMA((8,)),
            pltpu.SemaphoreType.DMA((7,)),
            pltpu.SemaphoreType.DMA((7,)),
        ],
        compiler_params=pltpu.CompilerParams(
            vmem_limit_bytes=56 * 2**20, collective_id=0, has_side_effects=True
        ),
    )(jnp.swapaxes(source_ids, 1, 2), valid_counts, x, wc, wq, wk, wv, wo, bias[None], gq[None], gk[None])
    return out[None]


def solution(mesh):
    return jax.shard_map(
        shards,
        mesh=mesh,
        in_specs=(P("frame", "row", None, None),)
        + (P(),) * 8
        + (P("frame", "row", None), P("frame", "row")),
        out_specs=P("frame", "row", None, None),
        check_vma=False,
    )
```

profile of v0, /device:TPU:26, one launch (start us, length us, event | category | flops | bytes accessed | tf_op | source)
XLA Modules:
  0.0 33.1 jit_solution(4351823629947501260)
XLA Ops:
  0.0 31.0 %shard_map.109 = bf16[6,128,512]{2,1,0:T(8,128)(2,1)} custom-call(s32[1,4,6]{2,1,0:T(4,128)} %bitcast.8, s32[1,6]{1,0:T(1,128)} %valid.1, bf16[6,128,512]{2,1,0:T(8,128)(2,1)} %bitcast.7, bf16[3,3,512,512]{3,2,1,0:T(8,128)(2,1)} %wc_hbm.1, bf16[512,512]{1,0:T(8,128)(2,1)} %wq_hbm.1, bf16[512,512]{1,0:T(8,128)(2,1)} %wk_hbm.1, bf16[512,512]{1,0:T(8,128)(2,1)} %wv_hbm.1, ...), custom_call_target="tpu_custom_call" | custom-call | tf_op jit(solution)/shard_map/pallas_call | solution.py:320
  31.0 2.1 %copy.13 = bf16[1,6,128,512]{3,2,1,0:T(8,128)(2,1)} copy(bf16[1,6,128,512]{3,2,1,0:T(8,128)(2,1)} %bitcast.6) | data formatting | bytes 1572864
where the time goes:
time: 33.3 us; the launch traced here: 33.1 us
  Pallas kernels  31 us (93%)
  local copies, waits for them, and re-layouts  2.1 us (6%)
    pallas_call x1, Pallas kernels, shards(): pl.pallas_call(kernel, out_shape=jax.ShapeDtypeStruct((rows, width, chans...  31 us
    unnamed x1, local copies, waits for them, and re-layouts  2.1 us

commit v1 on v0

v1 whole, which is shorter than its diff:
```python
import jax
import jax.numpy as jnp
from jax import lax
from jax.experimental import pallas as pl
from jax.experimental.pallas import tpu as pltpu
from jax.sharding import PartitionSpec as P

HD = 64
KSRC = 4
DISP = 2
GROUP = 4
LANES = GROUP * HD
LOG2E = 1.4426950408889634
F32 = jnp.float32
BF16 = jnp.bfloat16


def dot(a, b):
    return jnp.dot(a, b, preferred_element_type=F32)


def shift_columns(left, mid, right, width):
    count = mid.shape[0]
    col = lax.broadcasted_iota(jnp.int32, mid.shape, 0) % width
    return (
        mid
        + jnp.where(col == 0, 0.0, pltpu.roll(left, 1, 0))
        + jnp.where(col == width - 1, 0.0, pltpu.roll(right, count - 1, 0))
    )


def kernel(
    ids, valid, x, wc_hbm, wq_hbm, wk_hbm, wv_hbm, wo_hbm, bias, gq, gk,
    out,
    ext, wc, wq, wk, wv, wo, feats, reach, q, kdiag, vdiag, parts, acc, sums, mean, ones,
    local_sem, send_sem, recv_sem,
):
    rows, width, chans = x.shape
    groups = chans // LANES
    frame, band = lax.axis_index("frame"), lax.axis_index("row")
    frames, bands = lax.axis_size("frame"), lax.axis_size("row")
    has_prev, has_next = frame > 0, frame < frames - 1
    has_above, has_below = band > 0, band < bands - 1
    to_above, to_below, to_next = {"row": band - 1}, {"row": band + 1}, {"frame": frame + 1}

    def fetch(i, src, dst):
        return pltpu.make_async_copy(src, dst, local_sem.at[i])

    def send(i, src, dst, device):
        return pltpu.make_async_remote_copy(
            src_ref=src,
            dst_ref=dst,
            send_sem=send_sem.at[i],
            recv_sem=recv_sem.at[i],
            device_id=device,
            device_id_type=pl.DeviceIdType.MESH,
        )

    barrier = pltpu.get_barrier_semaphore()
    met = 0
    for there, device in (
        (has_above, to_above),
        (has_below, to_below),
        (has_prev, {"frame": frame - 1}),
        (has_next, to_next),
    ):
        met = met + there.astype(jnp.int32)

        @pl.when(there)
        def _():
            pl.semaphore_signal(
                barrier, inc=1, device_id=device, device_id_type=pl.DeviceIdType.MESH
            )

    load_x = fetch(0, x, ext.at[pl.ds(1, rows)])
    load_x.start()
    taps = [fetch(1 + b, wc_hbm.at[:, b], wc.at[b]) for b in range(3)]
    mats = [
        fetch(4 + i, src, dst)
        for i, (src, dst) in enumerate(
            ((wq_hbm, wq), (wk_hbm, wk), (wv_hbm, wv), (wo_hbm, wo))
        )
    ]
    for copy in taps:
        copy.start()

    kdiag[...] = jnp.zeros(kdiag.shape, BF16)
    vdiag[...] = jnp.zeros(vdiag.shape, BF16)
    row = lax.broadcasted_iota(jnp.int32, (LANES, LANES), 0) // HD
    col = lax.broadcasted_iota(jnp.int32, (LANES, LANES), 1) // HD
    mean[...] = jnp.where(row == col, 1.0 / HD, 0.0).astype(BF16)
    row = lax.broadcasted_iota(jnp.int32, (GROUP * width, LANES), 0) // width
    col = lax.broadcasted_iota(jnp.int32, (GROUP * width, LANES), 1) // HD
    ones[...] = jnp.where(row == col, 1.0, 0.0).astype(BF16)

    blank = jnp.zeros((width, chans), BF16)

    @pl.when(band == 0)
    def _():
        ext[0] = blank
        for i in range(DISP):
            reach[i] = blank

    @pl.when(band == bands - 1)
    def _():
        ext[rows + 1] = blank
        for i in range(DISP):
            reach[DISP + rows + i] = blank

    @pl.when(frame == 0)
    def _():
        for i in range(rows + 2 * DISP):
            reach[i] = blank

    pl.semaphore_wait(barrier, met)

    halo_up = send(0, x.at[0], ext.at[rows + 1], to_above)
    halo_down = send(1, x.at[rows - 1], ext.at[0], to_below)

    @pl.when(has_above)
    def _():
        halo_up.start()

    @pl.when(has_below)
    def _():
        halo_down.start()

    moves = [
        send(2 + r, feats.at[r], reach.at[DISP + r], to_next) for r in range(rows)
    ]
    relays = {}
    for i in range(DISP):
        relays[i] = (
            send(2 + rows + i, reach.at[DISP + i], reach.at[DISP + rows + i], to_above),
            has_above,
            has_below,
            DISP + rows + i,
        )
        r = rows - DISP + i
        relays[r] = (
            send(2 + rows + DISP + i, reach.at[DISP + r], reach.at[i], to_below),
            has_below,
            has_above,
            i,
        )

    chunks = [(1, rows - 2), (0, rows - 1)] + [
        tuple(range(r, min(r + 2, rows - DISP))) for r in range(DISP, rows - DISP, 2)
    ]

    load_x.wait()
    for i, chunk in enumerate(chunks):
        if i == 1:

            @pl.when(has_above)
            def _():
                halo_down.wait_recv()

            @pl.when(has_below)
            def _():
                halo_up.wait_recv()

        size = len(chunk) * width
        for b in range(3):
            if i == 0:
                taps[b].wait()
            window = jnp.concatenate(
                [jnp.concatenate([ext[r + a] for r in chunk], axis=0) for a in range(3)],
                axis=1,
            )
            parts[b, 0:size] = dot(window, wc[b].reshape(3 * chans, chans))
        total = shift_columns(parts[0, 0:size], parts[1, 0:size], parts[2, 0:size], width)
        total = (total + bias[...]).astype(BF16)
        for j, r in enumerate(chunk):
            feats[r] = total[j * width : (j + 1) * width]

        @pl.when(has_next)
        def _():
            for r in chunk:
                moves[r].start()

        if i == 0:
            for copy in mats:
                copy.start()

    def normed(flat, weight, gain):
        proj = dot(flat, weight[...])
        square = (proj * proj).astype(BF16)
        square = jnp.concatenate(
            [dot(square[:, g * LANES : (g + 1) * LANES], mean[...]) for g in range(groups)],
            axis=1,
        )
        return (proj * lax.rsqrt(square + 1e-06) * gain).astype(BF16)

    half = lax.broadcasted_iota(jnp.int32, (width, 2 * HD), 1) // HD

    def diagonal(ref, slot, value):
        for g in range(groups):
            for h in range(GROUP):
                lane = g * LANES + h // 2 * 2 * HD
                tile = value[:, lane : lane + 2 * HD]
                lane = h // 2 * 2 * HD
                ref[slot, g, h * width : (h + 1) * width, lane : lane + 2 * HD] = jnp.where(
                    half == h % 2, tile, jnp.zeros_like(tile)
                )

    def source(slot, flat):
        diagonal(kdiag, slot, normed(flat, wk, gk[...]))
        diagonal(vdiag, slot, dot(flat, wv[...]).astype(BF16))

    def attend(slot, first, last, counts):
        span = slice(first * width, last * width)
        for g in range(groups):
            lanes = slice(g * LANES, (g + 1) * LANES)
            expo = jnp.exp2(
                lax.dot_general(
                    q[span, lanes],
                    kdiag[slot, g],
                    (((1,), (1,)), ((), ())),
                    preferred_element_type=F32,
                )
            )
            if counts is not None:
                expo = jnp.concatenate(
                    [
                        expo[i * width : (i + 1) * width] * count
                        for i, count in enumerate(counts)
                    ],
                    axis=0,
                )
            mixed = dot(expo.astype(BF16), vdiag[slot, g])
            if counts is None:
                sums[g, span] = expo
                acc[span, lanes] = mixed
            else:
                sums[g, span] = sums[g, span] + expo
                acc[span, lanes] = acc[span, lanes] + mixed

    for copy in mats:
        copy.wait()
    flat = feats[...].reshape(rows * width, chans)
    q[...] = normed(flat, wq, gq[...] * (LOG2E * HD**-0.5))

    for n in range(rows):
        source(n % 2, feats[n])
        attend(n % 2, n, n + 1, None)

    live = has_prev.astype(jnp.int32)

    def named(n, place):
        count = 0
        for j in range(KSRC):
            here = ids[0, j, n] == band * rows + place - DISP
            count = count + (here & (j < valid[0, n])).astype(jnp.int32)
        return (count * live).astype(F32)

    def stage(k, place):
        first, last = max(place - 2 * DISP, 0), min(place, rows - 1) + 1
        source(k % 2, reach[place])
        attend(k % 2, first, last, [named(n, place) for n in range(first, last)])

    order = [r for chunk in chunks for r in chunk]
    k = 0
    late = []

    def pop(limit):
        nonlocal k
        while len(late) > limit:
            r = late.pop(0)
            relay, _, arriving, place = relays[r]

            @pl.when(has_prev & arriving)
            def _():
                relay.wait_recv()

            stage(k, place)
            k += 1

    for r in order:

        @pl.when(has_prev)
        def _():
            moves[r].wait_recv()

        if r in relays:
            relay, leaving, _, _ = relays[r]

            @pl.when(has_prev & leaving)
            def _():
                relay.start()

        stage(k, DISP + r)
        k += 1
        if r in relays:
            late.append(r)
        else:
            pop(0)
        pop(1)

    total = jnp.concatenate(
        [dot(sums[g].astype(BF16), ones[...]) for g in range(groups)], axis=1
    )
    mixed = (acc[...] * (1.0 / total)).astype(BF16)
    flat = feats[...].reshape(rows * width, chans).astype(F32)
    out[...] = (flat + dot(mixed, wo[...])).astype(BF16).reshape(rows, width, chans)

    @pl.when(has_above)
    def _():
        halo_up.wait_send()

    @pl.when(has_below)
    def _():
        halo_down.wait_send()

    @pl.when(has_next)
    def _():
        for copy in moves:
            copy.wait_send()

    for relay, leaving, _, _ in relays.values():

        @pl.when(has_prev & leaving)
        def _():
            relay.wait_send()


VM = pl.BlockSpec(memory_space=pltpu.VMEM)
SM = pl.BlockSpec(memory_space=pltpu.SMEM)
ANY = pl.BlockSpec(memory_space=pl.ANY)


def shards(x, wc, bias, wq, wk, wv, wo, gq, gk, source_ids, valid_counts):
    x = x[0]
    rows, width, chans = x.shape
    groups = chans // LANES
    square = pltpu.VMEM((chans, chans), BF16)

    def stack(count):
        return pltpu.VMEM((count, width, chans), BF16)

    links = 2 + rows + 2 * DISP
    out = pl.pallas_call(
        kernel,
        out_shape=jax.ShapeDtypeStruct((rows, width, chans), BF16),
        in_specs=[SM, SM] + [ANY] * 6 + [VM] * 3,
        out_specs=VM,
        scratch_shapes=[
            stack(rows + 2),
            pltpu.VMEM(wc.shape, BF16),
            square,
            square,
            square,
            square,
            stack(rows),
            stack(rows + 2 * DISP),
            pltpu.VMEM((rows * width, chans), BF16),
            pltpu.VMEM((2, groups, GROUP * width, LANES), BF16),
            pltpu.VMEM((2, groups, GROUP * width, LANES), BF16),
            pltpu.VMEM((3, 2 * width, chans), F32),
            pltpu.VMEM((rows * width, chans), F32),
            pltpu.VMEM((groups, rows * width, GROUP * width), F32),
            pltpu.VMEM((LANES, LANES), BF16),
            pltpu.VMEM((GROUP * width, LANES), BF16),
            pltpu.SemaphoreType.DMA((8,)),
            pltpu.SemaphoreType.DMA((links,)),
            pltpu.SemaphoreType.DMA((links,)),
        ],
        compiler_params=pltpu.CompilerParams(
            vmem_limit_bytes=56 * 2**20, collective_id=0, has_side_effects=True
        ),
    )(jnp.swapaxes(source_ids, 1, 2), valid_counts, x, wc, wq, wk, wv, wo, bias[None], gq[None], gk[None])
    return out[None]


def solution(mesh):
    return jax.shard_map(
        shards,
        mesh=mesh,
        in_specs=(P("frame", "row", None, None),)
        + (P(),) * 8
        + (P("frame", "row", None), P("frame", "row")),
        out_specs=P("frame", "row", None, None),
        check_vma=False,
    )
```

time: 33.3 us -> 30.8 us (0.925)
  the two profiles are of different devices: /device:TPU:26 before, /device:TPU:25 now
where the time goes in v1:
time: 30.8 us; the launch traced here: 30.6 us
  Pallas kernels  28.5 us (93%)
  local copies, waits for them, and re-layouts  2.1 us (7%)
    pallas_call x1, Pallas kernels, shards(): pl.pallas_call(kernel, out_shape=jax.ShapeDtypeStruct((rows, width, chans...  28.5 us
    unnamed x1, local copies, waits for them, and re-layouts  2.1 us

profile of v1, /device:TPU:25, one launch (start us, length us, event | category | flops | bytes accessed | tf_op | source)
XLA Modules:
  0.0 30.6 jit_solution(1428520611571323983)
XLA Ops:
  0.0 28.5 %shard_map.109 = bf16[6,128,512]{2,1,0:T(8,128)(2,1)} custom-call(s32[1,4,6]{2,1,0:T(4,128)} %bitcast.8, s32[1,6]{1,0:T(1,128)} %valid.1, bf16[6,128,512]{2,1,0:T(8,128)(2,1)} %bitcast.7, bf16[3,3,512,512]{3,2,1,0:T(8,128)(2,1)} %wc_hbm.1, bf16[512,512]{1,0:T(8,128)(2,1)} %wq_hbm.1, bf16[512,512]{1,0:T(8,128)(2,1)} %wk_hbm.1, bf16[512,512]{1,0:T(8,128)(2,1)} %wv_hbm.1, ...), custom_call_target="tpu_custom_call" | custom-call | tf_op jit(solution)/shard_map/pallas_call | solution.py:342
  28.5 2.1 %copy.13 = bf16[1,6,128,512]{3,2,1,0:T(8,128)(2,1)} copy(bf16[1,6,128,512]{3,2,1,0:T(8,128)(2,1)} %bitcast.6) | data formatting | bytes 1572864

commit v2 on v1

--- a/solution.py
+++ b/solution.py
@@ -32,7 +32,7 @@
 def kernel(
     ids, valid, x, wc_hbm, wq_hbm, wk_hbm, wv_hbm, wo_hbm, bias, gq, gk,
     out,
-    ext, wc, wq, wk, wv, wo, feats, reach, q, kdiag, vdiag, parts, acc, sums, mean, ones,
+    ext, wc, wq, wk, wv, wo, feats, reach, q, keys, values, kdiag, vdiag, parts, acc, sums, mean, ones,
     local_sem, send_sem, recv_sem,
 ):
     rows, width, chans = x.shape
@@ -144,25 +144,13 @@
             i,
         )
 
-    chunks = [(1, rows - 2), (0, rows - 1)] + [
-        tuple(range(r, min(r + 2, rows - DISP))) for r in range(DISP, rows - DISP, 2)
-    ]
-
-    load_x.wait()
-    for i, chunk in enumerate(chunks):
-        if i == 1:
-
-            @pl.when(has_above)
-            def _():
-                halo_down.wait_recv()
-
-            @pl.when(has_below)
-            def _():
-                halo_up.wait_recv()
-
+    edges = [(1, rows - 2), (0, rows - 1)]
+    inner = [tuple(range(r, min(r + 2, rows - DISP))) for r in range(DISP, rows - DISP, 2)]
+
+    def convolve(chunk, first):
         size = len(chunk) * width
         for b in range(3):
-            if i == 0:
+            if first:
                 taps[b].wait()
             window = jnp.concatenate(
                 [jnp.concatenate([ext[r + a] for r in chunk], axis=0) for a in range(3)],
@@ -174,14 +162,11 @@
         for j, r in enumerate(chunk):
             feats[r] = total[j * width : (j + 1) * width]
 
+    def forward(chunk):
         @pl.when(has_next)
         def _():
             for r in chunk:
                 moves[r].start()
-
-        if i == 0:
-            for copy in mats:
-                copy.start()
 
     def normed(flat, weight, gain):
         proj = dot(flat, weight[...])
@@ -203,10 +188,6 @@
                 ref[slot, g, h * width : (h + 1) * width, lane : lane + 2 * HD] = jnp.where(
                     half == h % 2, tile, jnp.zeros_like(tile)
                 )
-
-    def source(slot, flat):
-        diagonal(kdiag, slot, normed(flat, wk, gk[...]))
-        diagonal(vdiag, slot, dot(flat, wv[...]).astype(BF16))
 
     def attend(slot, first, last, counts):
         span = slice(first * width, last * width)
@@ -236,14 +217,44 @@
                 sums[g, span] = sums[g, span] + expo
                 acc[span, lanes] = acc[span, lanes] + mixed
 
+    def project(first, last):
+        span = slice(first * width, last * width)
+        flat = feats[first:last].reshape((last - first) * width, chans)
+        q[span] = normed(flat, wq, gq[...] * (LOG2E * HD**-0.5))
+        keys[span] = normed(flat, wk, gk[...])
+        values[span] = dot(flat, wv[...]).astype(BF16)
+
+    load_x.wait()
+    convolve(edges[0], True)
+    forward(edges[0])
+    for copy in mats:
+        copy.start()
+    for chunk in inner:
+        convolve(chunk, False)
     for copy in mats:
         copy.wait()
-    flat = feats[...].reshape(rows * width, chans)
-    q[...] = normed(flat, wq, gq[...] * (LOG2E * HD**-0.5))
-
+    project(1, rows - 1)
+
+    @pl.when(has_above)
+    def _():
+        halo_down.wait_recv()
+
+    @pl.when(has_below)
+    def _():
+        halo_up.wait_recv()
+
+    convolve(edges[1], False)
+    forward(edges[1])
+    for chunk in inner:
+        forward(chunk)
+    for r in edges[1]:
+        project(r, r + 1)
+    slots = kdiag.shape[0]
     for n in range(rows):
-        source(n % 2, feats[n])
-        attend(n % 2, n, n + 1, None)
+        span = slice(n * width, (n + 1) * width)
+        diagonal(kdiag, n % slots, keys[span])
+        diagonal(vdiag, n % slots, values[span])
+        attend(n % slots, n, n + 1, None)
 
     live = has_prev.astype(jnp.int32)
 
@@ -254,48 +265,44 @@
             count = count + (here & (j < valid[0, n])).astype(jnp.int32)
         return (count * live).astype(F32)
 
-    def stage(k, place):
-        first, last = max(place - 2 * DISP, 0), min(place, rows - 1) + 1
-        source(k % 2, reach[place])
-        attend(k % 2, first, last, [named(n, place) for n in range(first, last)])
-
-    order = [r for chunk in chunks for r in chunk]
-    k = 0
+    def stages(places, k):
+        flat = jnp.concatenate([reach[place] for place in places], axis=0)
+        key = normed(flat, wk, gk[...])
+        value = dot(flat, wv[...]).astype(BF16)
+        for i, place in enumerate(places):
+            slot = (k + i) % slots
+            first, last = max(place - 2 * DISP, 0), min(place, rows - 1) + 1
+            diagonal(kdiag, slot, key[i * width : (i + 1) * width])
+            diagonal(vdiag, slot, value[i * width : (i + 1) * width])
+            attend(slot, first, last, [named(n, place) for n in range(first, last)])
+
     late = []
-
-    def pop(limit):
-        nonlocal k
-        while len(late) > limit:
-            r = late.pop(0)
-            relay, _, arriving, place = relays[r]
+    for i, r in enumerate([r for chunk in edges + inner for r in chunk]):
+
+        @pl.when(has_prev)
+        def _():
+            moves[r].wait_recv()
+
+        if r in relays:
+            relay, leaving, _, _ = relays[r]
+
+            @pl.when(has_prev & leaving)
+            def _():
+                relay.start()
+
+        places = [DISP + r]
+        if late:
+            relay, arriving, place = late.pop(0)
 
             @pl.when(has_prev & arriving)
             def _():
                 relay.wait_recv()
 
-            stage(k, place)
-            k += 1
-
-    for r in order:
-
-        @pl.when(has_prev)
-        def _():
-            moves[r].wait_recv()
-
+            places.append(place)
+        stages(places, 2 * i)
         if r in relays:
-            relay, leaving, _, _ = relays[r]
-
-            @pl.when(has_prev & leaving)
-            def _():
-                relay.start()
-
-        stage(k, DISP + r)
-        k += 1
-        if r in relays:
-            late.append(r)
-        else:
-            pop(0)
-        pop(1)
+            relay, _, arriving, place = relays[r]
+            late.append((relay, arriving, place))
 
     total = jnp.concatenate(
         [dot(sums[g].astype(BF16), ones[...]) for g in range(groups)], axis=1
@@ -354,8 +361,10 @@
             stack(rows),
             stack(rows + 2 * DISP),
             pltpu.VMEM((rows * width, chans), BF16),
-            pltpu.VMEM((2, groups, GROUP * width, LANES), BF16),
-            pltpu.VMEM((2, groups, GROUP * width, LANES), BF16),
+            pltpu.VMEM((rows * width, chans), BF16),
+            pltpu.VMEM((rows * width, chans), BF16),
+            pltpu.VMEM((4, groups, GROUP * width, LANES), BF16),
+            pltpu.VMEM((4, groups, GROUP * width, LANES), BF16),
             pltpu.VMEM((3, 2 * width, chans), F32),
             pltpu.VMEM((rows * width, chans), F32),
             pltpu.VMEM((groups, rows * width, GROUP * width), F32),

time: 30.8 us -> 29.8 us (0.968)
  the two profiles are of different devices: /device:TPU:25 before, /device:TPU:26 now
where the time goes in v2:
time: 29.8 us; the launch traced here: 29.6 us
  Pallas kernels  27.5 us (92%)
  local copies, waits for them, and re-layouts  2.1 us (7%)
    pallas_call x1, Pallas kernels, shards(): pl.pallas_call(kernel, out_shape=jax.ShapeDtypeStruct((rows, width, chans...  27.5 us
    unnamed x1, local copies, waits for them, and re-layouts  2.1 us

profile of v2, /device:TPU:26, one launch (start us, length us, event | category | flops | bytes accessed | tf_op | source)
XLA Modules:
  0.0 29.6 jit_solution(7576980707851312434)
XLA Ops:
  0.0 27.5 %shard_map.109 = bf16[6,128,512]{2,1,0:T(8,128)(2,1)} custom-call(s32[1,4,6]{2,1,0:T(4,128)} %bitcast.8, s32[1,6]{1,0:T(1,128)} %valid.1, bf16[6,128,512]{2,1,0:T(8,128)(2,1)} %bitcast.7, bf16[3,3,512,512]{3,2,1,0:T(8,128)(2,1)} %wc_hbm.1, bf16[512,512]{1,0:T(8,128)(2,1)} %wq_hbm.1, bf16[512,512]{1,0:T(8,128)(2,1)} %wk_hbm.1, bf16[512,512]{1,0:T(8,128)(2,1)} %wv_hbm.1, ...), custom_call_target="tpu_custom_call" | custom-call | tf_op jit(solution)/shard_map/pallas_call | solution.py:349
  27.5 2.1 %copy.13 = bf16[1,6,128,512]{3,2,1,0:T(8,128)(2,1)} copy(bf16[1,6,128,512]{3,2,1,0:T(8,128)(2,1)} %bitcast.6) | data formatting | bytes 1572864

commit v3 on v2

--- a/solution.py
+++ b/solution.py
@@ -30,9 +30,9 @@
 
 
 def kernel(
-    ids, valid, x, wc_hbm, wq_hbm, wk_hbm, wv_hbm, wo_hbm, bias, gq, gk,
-    out,
-    ext, wc, wq, wk, wv, wo, feats, reach, q, keys, values, kdiag, vdiag, parts, acc, sums, mean, ones,
+    ids, valid, x, wc_hbm, wq_hbm, wk_hbm, wv_hbm, bias, gq, gk,
+    feats, attended,
+    ext, wc, wq, wk, wv, reach, q, keys, values, kdiag, vdiag, parts, acc, sums, mean, ones,
     local_sem, send_sem, recv_sem,
 ):
     rows, width, chans = x.shape
@@ -78,7 +78,7 @@
     mats = [
         fetch(4 + i, src, dst)
         for i, (src, dst) in enumerate(
-            ((wq_hbm, wq), (wk_hbm, wk), (wv_hbm, wv), (wo_hbm, wo))
+            ((wq_hbm, wq), (wk_hbm, wk), (wv_hbm, wv))
         )
     ]
     for copy in taps:
@@ -191,6 +191,7 @@
 
     def attend(slot, first, last, counts):
         span = slice(first * width, last * width)
+        probs = []
         for g in range(groups):
             lanes = slice(g * LANES, (g + 1) * LANES)
             expo = jnp.exp2(
@@ -201,7 +202,9 @@
                     preferred_element_type=F32,
                 )
             )
-            if counts is not None:
+            if counts is None:
+                sums[g, span] = expo
+            else:
                 expo = jnp.concatenate(
                     [
                         expo[i * width : (i + 1) * width] * count
@@ -209,13 +212,15 @@
                     ],
                     axis=0,
                 )
-            mixed = dot(expo.astype(BF16), vdiag[slot, g])
+                sums[g, span] = sums[g, span] + expo
+            probs.append(expo.astype(BF16))
+        mixed = [dot(probs[g], vdiag[slot, g]) for g in range(groups)]
+        for g in range(groups):
+            lanes = slice(g * LANES, (g + 1) * LANES)
             if counts is None:
-                sums[g, span] = expo
-                acc[span, lanes] = mixed
+                acc[span, lanes] = mixed[g]
             else:
-                sums[g, span] = sums[g, span] + expo
-                acc[span, lanes] = acc[span, lanes] + mixed
+                acc[span, lanes] = acc[span, lanes] + mixed[g]
 
     def project(first, last):
         span = slice(first * width, last * width)
@@ -307,9 +312,7 @@
     total = jnp.concatenate(
         [dot(sums[g].astype(BF16), ones[...]) for g in range(groups)], axis=1
     )
-    mixed = (acc[...] * (1.0 / total)).astype(BF16)
-    flat = feats[...].reshape(rows * width, chans).astype(F32)
-    out[...] = (flat + dot(mixed, wo[...])).astype(BF16).reshape(rows, width, chans)
+    attended[...] = (acc[...] * (1.0 / total)).astype(BF16).reshape(rows, width, chans)
 
     @pl.when(has_above)
     def _():
@@ -331,9 +334,20 @@
             relay.wait_send()
 
 
+def join(feats, attended, wo, out, stage, sem):
+    rows, width, chans = feats.shape
+    copies = []
+    for r in range(rows):
+        stage[r] = (feats[r].astype(F32) + dot(attended[r], wo[...])).astype(BF16)
+        copies.append(pltpu.make_async_copy(stage.at[r], out.at[r], sem.at[r]))
+        copies[r].start()
+    for copy in copies:
+        copy.wait()
+
+
 VM = pl.BlockSpec(memory_space=pltpu.VMEM)
 SM = pl.BlockSpec(memory_space=pltpu.SMEM)
-ANY = pl.BlockSpec(memory_space=pl.ANY)
+ANY = pl.BlockSpec(memory_space=pltpu.HBM)
 
 
 def shards(x, wc, bias, wq, wk, wv, wo, gq, gk, source_ids, valid_counts):
@@ -346,19 +360,18 @@
         return pltpu.VMEM((count, width, chans), BF16)
 
     links = 2 + rows + 2 * DISP
-    out = pl.pallas_call(
+    shape = jax.ShapeDtypeStruct((rows, width, chans), BF16)
+    feats, attended = pl.pallas_call(
         kernel,
-        out_shape=jax.ShapeDtypeStruct((rows, width, chans), BF16),
-        in_specs=[SM, SM] + [ANY] * 6 + [VM] * 3,
-        out_specs=VM,
+        out_shape=(pltpu.VMEM(shape.shape, BF16), pltpu.VMEM(shape.shape, BF16)),
+        in_specs=[SM, SM] + [ANY] * 5 + [VM] * 3,
+        out_specs=(VM, VM),
         scratch_shapes=[
             stack(rows + 2),
             pltpu.VMEM(wc.shape, BF16),
             square,
             square,
             square,
-            square,
-            stack(rows),
             stack(rows + 2 * DISP),
             pltpu.VMEM((rows * width, chans), BF16),
             pltpu.VMEM((rows * width, chans), BF16),
@@ -377,7 +390,18 @@
         compiler_params=pltpu.CompilerParams(
             vmem_limit_bytes=56 * 2**20, collective_id=0, has_side_effects=True
         ),
-    )(jnp.swapaxes(source_ids, 1, 2), valid_counts, x, wc, wq, wk, wv, wo, bias[None], gq[None], gk[None])
+    )(jnp.swapaxes(source_ids, 1, 2), valid_counts, x, wc, wq, wk, wv, bias[None], gq[None], gk[None])
+    out = pl.pallas_call(
+        join,
+        out_shape=shape,
+        in_specs=[VM] * 3,
+        out_specs=ANY,
+        scratch_shapes=[
+            pltpu.VMEM((rows, width, chans), BF16),
+            pltpu.SemaphoreType.DMA((rows,)),
+        ],
+        compiler_params=pltpu.CompilerParams(vmem_limit_bytes=12 * 2**20),
+    )(feats, attended, wo)
     return out[None]
 
 

time: 29.8 us -> 27 us (0.906)
  local copies, waits for them, and re-layouts: 2.1 us -> 0.01 us
  Pallas kernels: 27.5 us -> 26.7 us
    unnamed x1 -> x2, local copies, waits for them, and re-layouts: 2.1 us -> 0.01 us
    pallas_call x1 -> x2, Pallas kernels: 27.5 us -> 26.7 us  [the longest x1 25.4 us: shards(): pl.pallas_call(kernel, out_shape=(pltpu.VMEM(shape.shape, BF16), pltpu.VM...]
where the time goes in v3:
time: 27 us; the launch traced here: 26.7 us
  Pallas kernels  26.7 us (99%)
    pallas_call x1, Pallas kernels, shards(): pl.pallas_call(kernel, out_shape=(pltpu.VMEM(shape.shape, BF16), pltpu.VM...  25.4 us
    pallas_call x1, Pallas kernels, shards(): pl.pallas_call(join, out_shape=shape, in_specs=[VM] * 3, out_specs=ANY, s...  1.3 us

profile of v3, /device:TPU:26, one launch (start us, length us, event | category | flops | bytes accessed | tf_op | source)
XLA Modules:
  0.0 26.7 jit_solution(620776937585658099)
XLA Ops:
  0.0 0.0 copy-start
  0.0 25.4 %shard_map.109 = (bf16[6,128,512]{2,1,0:T(8,128)(2,1)S(1)}, bf16[6,128,512]{2,1,0:T(8,128)(2,1)S(1)}) custom-call(s32[1,4,6]{2,1,0:T(4,128)} %bitcast.7, s32[1,6]{1,0:T(1,128)} %valid.1, bf16[6,128,512]{2,1,0:T(8,128)(2,1)} %bitcast.6, bf16[3,3,512,512]{3,2,1,0:T(8,128)(2,1)} %wc_hbm.1, bf16[512,512]{1,0:T(8,128)(2,1)} %wq_hbm.1, bf16[512,512]{1,0:T(8,128)(2,1)} %wk_hbm.1, ...), custom_call_target="tpu_custom_call" | custom-call | tf_op jit(solution)/shard_map/pallas_call | solution.py:364
  25.4 0.0 copy-done
  25.4 1.3 %shard_map.110 = bf16[6,128,512]{2,1,0:T(8,128)(2,1)} custom-call(bf16[6,128,512]{2,1,0:T(8,128)(2,1)S(1)} %get-tuple-element.7.feats, bf16[6,128,512]{2,1,0:T(8,128)(2,1)S(1)} %get-tuple-element.8.attended, bf16[512,512]{1,0:T(8,128)(2,1)S(1)} %copy-done), custom_call_target="tpu_custom_call" | custom-call | tf_op jit(solution)/shard_map/pallas_call | solution.py:394
Async XLA Ops:
  0.0 25.4 %copy-start = (bf16[512,512]{1,0:T(8,128)(2,1)S(1)}, bf16[512,512]{1,0:T(8,128)(2,1)}, u32[]{:S(2)}) copy-start(bf16[512,512]{1,0:T(8,128)(2,1)} %wo.1) | copy-start | bytes 1572868

commit v4 on v3

--- a/solution.py
+++ b/solution.py
@@ -32,7 +32,7 @@
 def kernel(
     ids, valid, x, wc_hbm, wq_hbm, wk_hbm, wv_hbm, bias, gq, gk,
     feats, attended,
-    ext, wc, wq, wk, wv, reach, q, keys, values, kdiag, vdiag, parts, acc, sums, mean, ones,
+    ext, wc, wq, wk, wv, reach, q, keys, values, kdiag, vdiag, parts, acc, sums, mean,
     local_sem, send_sem, recv_sem,
 ):
     rows, width, chans = x.shape
@@ -89,9 +89,6 @@
     row = lax.broadcasted_iota(jnp.int32, (LANES, LANES), 0) // HD
     col = lax.broadcasted_iota(jnp.int32, (LANES, LANES), 1) // HD
     mean[...] = jnp.where(row == col, 1.0 / HD, 0.0).astype(BF16)
-    row = lax.broadcasted_iota(jnp.int32, (GROUP * width, LANES), 0) // width
-    col = lax.broadcasted_iota(jnp.int32, (GROUP * width, LANES), 1) // HD
-    ones[...] = jnp.where(row == col, 1.0, 0.0).astype(BF16)
 
     blank = jnp.zeros((width, chans), BF16)
 
@@ -281,38 +278,56 @@
             diagonal(vdiag, slot, value[i * width : (i + 1) * width])
             attend(slot, first, last, [named(n, place) for n in range(first, last)])
 
+    side = lax.broadcasted_iota(jnp.int32, (width, 2 * HD), 1) // HD
+
+    def finish(n):
+        span = slice(n * width, (n + 1) * width)
+        for g in range(groups):
+            total = [
+                jnp.sum(sums[g, span, h * width : (h + 1) * width], axis=1, keepdims=True)
+                for h in range(GROUP)
+            ]
+            for h in range(0, GROUP, 2):
+                lanes = slice(g * LANES + h * HD, g * LANES + (h + 2) * HD)
+                inverse = 1.0 / jnp.where(side == 0, total[h], total[h + 1])
+                attended[n, :, lanes] = (acc[span, lanes] * inverse).astype(BF16)
+
+    steps = []
     late = []
-    for i, r in enumerate([r for chunk in edges + inner for r in chunk]):
-
-        @pl.when(has_prev)
-        def _():
-            moves[r].wait_recv()
-
-        if r in relays:
-            relay, leaving, _, _ = relays[r]
-
-            @pl.when(has_prev & leaving)
-            def _():
-                relay.start()
-
-        places = [DISP + r]
-        if late:
-            relay, arriving, place = late.pop(0)
-
-            @pl.when(has_prev & arriving)
-            def _():
-                relay.wait_recv()
-
-            places.append(place)
-        stages(places, 2 * i)
+    for r in [r for chunk in edges + inner for r in chunk]:
+        step = [(moves[r], None, DISP + r, r)]
+        if len(late) > 1:
+            step.append(late.pop(0))
+        steps.append(step)
         if r in relays:
             relay, _, arriving, place = relays[r]
-            late.append((relay, arriving, place))
-
-    total = jnp.concatenate(
-        [dot(sums[g].astype(BF16), ones[...]) for g in range(groups)], axis=1
-    )
-    attended[...] = (acc[...] * (1.0 / total)).astype(BF16).reshape(rows, width, chans)
+            late.append((relay, arriving, place, None))
+    steps[-1:-1] = [[entry] for entry in late]
+
+    left = [2 * DISP + 1] * rows
+    k = 0
+    for step in steps:
+        for copy, arriving, _, r in step:
+
+            @pl.when(has_prev if arriving is None else has_prev & arriving)
+            def _():
+                copy.wait_recv()
+
+            if r in relays:
+                relay, leaving, _, _ = relays[r]
+
+                @pl.when(has_prev & leaving)
+                def _():
+                    relay.start()
+
+        places = [place for _, _, place, _ in step]
+        stages(places, k)
+        k += len(places)
+        for place in places:
+            for n in range(max(place - 2 * DISP, 0), min(place, rows - 1) + 1):
+                left[n] -= 1
+                if left[n] == 0:
+                    finish(n)
 
     @pl.when(has_above)
     def _():
@@ -382,7 +397,6 @@
             pltpu.VMEM((rows * width, chans), F32),
             pltpu.VMEM((groups, rows * width, GROUP * width), F32),
             pltpu.VMEM((LANES, LANES), BF16),
-            pltpu.VMEM((GROUP * width, LANES), BF16),
             pltpu.SemaphoreType.DMA((8,)),
             pltpu.SemaphoreType.DMA((links,)),
             pltpu.SemaphoreType.DMA((links,)),

time: 27 us -> 27.1 us (level)
  no operation moved by 1% of the time
where the time goes in v4:
time: 27.1 us; the launch traced here: 27 us
  Pallas kernels  26.9 us (99%)
    pallas_call x1, Pallas kernels, shards(): pl.pallas_call(kernel, out_shape=(pltpu.VMEM(shape.shape, BF16), pltpu.VM...  25.6 us
    pallas_call x1, Pallas kernels, shards(): pl.pallas_call(join, out_shape=shape, in_specs=[VM] * 3, out_specs=ANY, s...  1.29 us

profile of v4, /device:TPU:26, one launch (start us, length us, event | category | flops | bytes accessed | tf_op | source)
XLA Modules:
  0.0 27.0 jit_solution(131382743628869028)
XLA Ops:
  0.0 0.0 copy-start
  0.0 25.6 %shard_map.109 = (bf16[6,128,512]{2,1,0:T(8,128)(2,1)S(1)}, bf16[6,128,512]{2,1,0:T(8,128)(2,1)S(1)}) custom-call(s32[1,4,6]{2,1,0:T(4,128)} %bitcast.7, s32[1,6]{1,0:T(1,128)} %valid.1, bf16[6,128,512]{2,1,0:T(8,128)(2,1)} %bitcast.6, bf16[3,3,512,512]{3,2,1,0:T(8,128)(2,1)} %wc_hbm.1, bf16[512,512]{1,0:T(8,128)(2,1)} %wq_hbm.1, bf16[512,512]{1,0:T(8,128)(2,1)} %wk_hbm.1, ...), custom_call_target="tpu_custom_call" | custom-call | tf_op jit(solution)/shard_map/pallas_call | solution.py:379
  25.6 0.0 copy-done
  25.7 1.3 %shard_map.110 = bf16[6,128,512]{2,1,0:T(8,128)(2,1)} custom-call(bf16[6,128,512]{2,1,0:T(8,128)(2,1)S(1)} %get-tuple-element.7.feats, bf16[6,128,512]{2,1,0:T(8,128)(2,1)S(1)} %get-tuple-element.8.attended, bf16[512,512]{1,0:T(8,128)(2,1)S(1)} %copy-done), custom_call_target="tpu_custom_call" | custom-call | tf_op jit(solution)/shard_map/pallas_call | solution.py:408
Async XLA Ops:
  0.0 25.6 %copy-start = (bf16[512,512]{1,0:T(8,128)(2,1)S(1)}, bf16[512,512]{1,0:T(8,128)(2,1)}, u32[]{:S(2)}) copy-start(bf16[512,512]{1,0:T(8,128)(2,1)} %wo.1) | copy-start | bytes 1572868

commit v5 on v4

--- a/solution.py
+++ b/solution.py
@@ -74,14 +74,22 @@
 
     load_x = fetch(0, x, ext.at[pl.ds(1, rows)])
     load_x.start()
-    taps = [fetch(1 + b, wc_hbm.at[:, b], wc.at[b]) for b in range(3)]
+    middle = chans // 2
+    halves = (pl.ds(0, middle), pl.ds(middle, middle))
+    taps = [
+        [
+            fetch(1 + 3 * i + b, wc_hbm.at[:, b, :, half], wc.at[b, :, :, half])
+            for b in range(3)
+        ]
+        for i, half in enumerate(halves)
+    ]
     mats = [
-        fetch(4 + i, src, dst)
+        fetch(7 + i, src, dst)
         for i, (src, dst) in enumerate(
             ((wq_hbm, wq), (wk_hbm, wk), (wv_hbm, wv))
         )
     ]
-    for copy in taps:
+    for copy in taps[0]:
         copy.start()
 
     kdiag[...] = jnp.zeros(kdiag.shape, BF16)
@@ -109,22 +117,22 @@
         for i in range(rows + 2 * DISP):
             reach[i] = blank
 
-    pl.semaphore_wait(barrier, met)
-
     halo_up = send(0, x.at[0], ext.at[rows + 1], to_above)
     halo_down = send(1, x.at[rows - 1], ext.at[0], to_below)
 
-    @pl.when(has_above)
-    def _():
-        halo_up.start()
-
-    @pl.when(has_below)
-    def _():
-        halo_down.start()
-
-    moves = [
-        send(2 + r, feats.at[r], reach.at[DISP + r], to_next) for r in range(rows)
-    ]
+    edges = [(1, rows - 2), (0, rows - 1)]
+    moves = []
+    for r in range(rows):
+        at = [2 + r]
+        if r in edges[0]:
+            at.append(2 + rows + 2 * DISP + edges[0].index(r))
+        cuts = halves if r in edges[0] else (pl.ds(0, chans),)
+        moves.append(
+            [
+                send(i, feats.at[r, :, cut], reach.at[DISP + r, :, cut], to_next)
+                for i, cut in zip(at, cuts)
+            ]
+        )
     relays = {}
     for i in range(DISP):
         relays[i] = (
@@ -141,29 +149,29 @@
             i,
         )
 
-    edges = [(1, rows - 2), (0, rows - 1)]
     inner = [tuple(range(r, min(r + 2, rows - DISP))) for r in range(DISP, rows - DISP, 2)]
 
-    def convolve(chunk, first):
+    def convolve(chunk, lanes):
         size = len(chunk) * width
         for b in range(3):
-            if first:
-                taps[b].wait()
             window = jnp.concatenate(
                 [jnp.concatenate([ext[r + a] for r in chunk], axis=0) for a in range(3)],
                 axis=1,
             )
-            parts[b, 0:size] = dot(window, wc[b].reshape(3 * chans, chans))
-        total = shift_columns(parts[0, 0:size], parts[1, 0:size], parts[2, 0:size], width)
-        total = (total + bias[...]).astype(BF16)
+            kernel_b = wc[b, :, :, lanes]
+            parts[b, 0:size, lanes] = dot(window, kernel_b.reshape(3 * chans, -1))
+        total = shift_columns(*(parts[b, 0:size, lanes] for b in range(3)), width)
+        total = (total + bias[:, lanes]).astype(BF16)
         for j, r in enumerate(chunk):
-            feats[r] = total[j * width : (j + 1) * width]
-
-    def forward(chunk):
+            feats[r, :, lanes] = total[j * width : (j + 1) * width]
+
+    whole = pl.ds(0, chans)
+
+    def forward(copies):
         @pl.when(has_next)
         def _():
-            for r in chunk:
-                moves[r].start()
+            for copy in copies:
+                copy.start()
 
     def normed(flat, weight, gain):
         proj = dot(flat, weight[...])
@@ -227,12 +235,29 @@
         values[span] = dot(flat, wv[...]).astype(BF16)
 
     load_x.wait()
-    convolve(edges[0], True)
-    forward(edges[0])
+    for b in range(3):
+        taps[0][b].wait()
+        taps[1][b].start()
+    convolve(edges[0], halves[0])
+    pl.semaphore_wait(barrier, met)
+    forward([moves[r][0] for r in edges[0]])
+
+    @pl.when(has_above)
+    def _():
+        halo_up.start()
+
+    @pl.when(has_below)
+    def _():
+        halo_down.start()
+
+    for copy in taps[1]:
+        copy.wait()
+    convolve(edges[0], halves[1])
+    forward([moves[r][1] for r in edges[0]])
     for copy in mats:
         copy.start()
     for chunk in inner:
-        convolve(chunk, False)
+        convolve(chunk, whole)
     for copy in mats:
         copy.wait()
     project(1, rows - 1)
@@ -245,10 +270,8 @@
     def _():
         halo_up.wait_recv()
 
-    convolve(edges[1], False)
-    forward(edges[1])
-    for chunk in inner:
-        forward(chunk)
+    convolve(edges[1], whole)
+    forward([copy for chunk in edges[1:] + inner for r in chunk for copy in moves[r]])
     for r in edges[1]:
         project(r, r + 1)
     slots = kdiag.shape[0]
@@ -301,17 +324,18 @@
         steps.append(step)
         if r in relays:
             relay, _, arriving, place = relays[r]
-            late.append((relay, arriving, place, None))
+            late.append(([relay], arriving, place, None))
     steps[-1:-1] = [[entry] for entry in late]
 
     left = [2 * DISP + 1] * rows
     k = 0
     for step in steps:
-        for copy, arriving, _, r in step:
+        for copies, arriving, _, r in step:
 
             @pl.when(has_prev if arriving is None else has_prev & arriving)
             def _():
-                copy.wait_recv()
+                for copy in copies:
+                    copy.wait_recv()
 
             if r in relays:
                 relay, leaving, _, _ = relays[r]
@@ -339,8 +363,9 @@
 
     @pl.when(has_next)
     def _():
-        for copy in moves:
-            copy.wait_send()
+        for copies in moves:
+            for copy in copies:
+                copy.wait_send()
 
     for relay, leaving, _, _ in relays.values():
 
@@ -374,7 +399,7 @@
     def stack(count):
         return pltpu.VMEM((count, width, chans), BF16)
 
-    links = 2 + rows + 2 * DISP
+    links = 4 + rows + 2 * DISP
     shape = jax.ShapeDtypeStruct((rows, width, chans), BF16)
     feats, attended = pl.pallas_call(
         kernel,
@@ -397,7 +422,7 @@
             pltpu.VMEM((rows * width, chans), F32),
             pltpu.VMEM((groups, rows * width, GROUP * width), F32),
             pltpu.VMEM((LANES, LANES), BF16),
-            pltpu.SemaphoreType.DMA((8,)),
+            pltpu.SemaphoreType.DMA((10,)),
             pltpu.SemaphoreType.DMA((links,)),
             pltpu.SemaphoreType.DMA((links,)),
         ],

time: 27.1 us -> 26.8 us (0.989)
  the two profiles are of different devices: /device:TPU:26 before, /device:TPU:9 now
where the time goes in v5:
time: 26.8 us; the launch traced here: 26.6 us
  Pallas kernels  26.6 us (99%)
    pallas_call x1, Pallas kernels, shards(): pl.pallas_call(kernel, out_shape=(pltpu.VMEM(shape.shape, BF16), pltpu.VM...  25.3 us
    pallas_call x1, Pallas kernels, shards(): pl.pallas_call(join, out_shape=shape, in_specs=[VM] * 3, out_specs=ANY, s...  1.3 us

profile of v5, /device:TPU:9, one launch (start us, length us, event | category | flops | bytes accessed | tf_op | source)
XLA Modules:
  0.0 26.6 jit_solution(15548799278643500529)
XLA Ops:
  0.0 0.0 copy-start
  0.0 25.3 %shard_map.109 = (bf16[6,128,512]{2,1,0:T(8,128)(2,1)S(1)}, bf16[6,128,512]{2,1,0:T(8,128)(2,1)S(1)}) custom-call(s32[1,4,6]{2,1,0:T(4,128)} %bitcast.7, s32[1,6]{1,0:T(1,128)} %valid.1, bf16[6,128,512]{2,1,0:T(8,128)(2,1)} %bitcast.6, bf16[3,3,512,512]{3,2,1,0:T(8,128)(2,1)} %wc_hbm.1, bf16[512,512]{1,0:T(8,128)(2,1)} %wq_hbm.1, bf16[512,512]{1,0:T(8,128)(2,1)} %wk_hbm.1, ...), custom_call_target="tpu_custom_call" | custom-call | tf_op jit(solution)/shard_map/pallas_call | solution.py:404
  25.3 0.0 copy-done
  25.3 1.3 %shard_map.110 = bf16[6,128,512]{2,1,0:T(8,128)(2,1)} custom-call(bf16[6,128,512]{2,1,0:T(8,128)(2,1)S(1)} %get-tuple-element.7.feats, bf16[6,128,512]{2,1,0:T(8,128)(2,1)S(1)} %get-tuple-element.8.attended, bf16[512,512]{1,0:T(8,128)(2,1)S(1)} %copy-done), custom_call_target="tpu_custom_call" | custom-call | tf_op jit(solution)/shard_map/pallas_call | solution.py:433
Async XLA Ops:
  0.0 25.3 %copy-start = (bf16[512,512]{1,0:T(8,128)(2,1)S(1)}, bf16[512,512]{1,0:T(8,128)(2,1)}, u32[]{:S(2)}) copy-start(bf16[512,512]{1,0:T(8,128)(2,1)} %wo.1) | copy-start | bytes 1572868

commit v6 on v5

--- a/solution.py
+++ b/solution.py
@@ -151,9 +151,11 @@
 
     inner = [tuple(range(r, min(r + 2, rows - DISP))) for r in range(DISP, rows - DISP, 2)]
 
-    def convolve(chunk, lanes):
+    def convolve(chunk, lanes, between=None):
         size = len(chunk) * width
         for b in range(3):
+            if b == 1 and between is not None:
+                between()
             window = jnp.concatenate(
                 [jnp.concatenate([ext[r + a] for r in chunk], axis=0) for a in range(3)],
                 axis=1,
@@ -238,17 +240,20 @@
     for b in range(3):
         taps[0][b].wait()
         taps[1][b].start()
-    convolve(edges[0], halves[0])
-    pl.semaphore_wait(barrier, met)
+
+    def greet():
+        pl.semaphore_wait(barrier, met)
+
+        @pl.when(has_above)
+        def _():
+            halo_up.start()
+
+        @pl.when(has_below)
+        def _():
+            halo_down.start()
+
+    convolve(edges[0], halves[0], greet)
     forward([moves[r][0] for r in edges[0]])
-
-    @pl.when(has_above)
-    def _():
-        halo_up.start()
-
-    @pl.when(has_below)
-    def _():
-        halo_down.start()
 
     for copy in taps[1]:
         copy.wait()

time: 26.8 us -> 26.4 us (0.985)
  the two profiles are of different devices: /device:TPU:9 before, /device:TPU:26 now
where the time goes in v6:
time: 26.4 us; the launch traced here: 26.2 us
  Pallas kernels  26.2 us (99%)
    pallas_call x1, Pallas kernels, shards(): pl.pallas_call(kernel, out_shape=(pltpu.VMEM(shape.shape, BF16), pltpu.VM...  24.9 us
    pallas_call x1, Pallas kernels, shards(): pl.pallas_call(join, out_shape=shape, in_specs=[VM] * 3, out_specs=ANY, s...  1.29 us

profile of v6, /device:TPU:26, one launch (start us, length us, event | category | flops | bytes accessed | tf_op | source)
XLA Modules:
  0.0 26.2 jit_solution(16972909033949370960)
XLA Ops:
  0.0 0.0 copy-start
  0.0 24.9 %shard_map.109 = (bf16[6,128,512]{2,1,0:T(8,128)(2,1)S(1)}, bf16[6,128,512]{2,1,0:T(8,128)(2,1)S(1)}) custom-call(s32[1,4,6]{2,1,0:T(4,128)} %bitcast.7, s32[1,6]{1,0:T(1,128)} %valid.1, bf16[6,128,512]{2,1,0:T(8,128)(2,1)} %bitcast.6, bf16[3,3,512,512]{3,2,1,0:T(8,128)(2,1)} %wc_hbm.1, bf16[512,512]{1,0:T(8,128)(2,1)} %wq_hbm.1, bf16[512,512]{1,0:T(8,128)(2,1)} %wk_hbm.1, ...), custom_call_target="tpu_custom_call" | custom-call | tf_op jit(solution)/shard_map/pallas_call | solution.py:409
  24.9 0.0 copy-done
  24.9 1.3 %shard_map.110 = bf16[6,128,512]{2,1,0:T(8,128)(2,1)} custom-call(bf16[6,128,512]{2,1,0:T(8,128)(2,1)S(1)} %get-tuple-element.7.feats, bf16[6,128,512]{2,1,0:T(8,128)(2,1)S(1)} %get-tuple-element.8.attended, bf16[512,512]{1,0:T(8,128)(2,1)S(1)} %copy-done), custom_call_target="tpu_custom_call" | custom-call | tf_op jit(solution)/shard_map/pallas_call | solution.py:438
Async XLA Ops:
  0.0 24.9 %copy-start = (bf16[512,512]{1,0:T(8,128)(2,1)S(1)}, bf16[512,512]{1,0:T(8,128)(2,1)}, u32[]{:S(2)}) copy-start(bf16[512,512]{1,0:T(8,128)(2,1)} %wo.1) | copy-start | bytes 1572868
